TPU v7x, 512 devices: a whole 4x4x16 slice. The times are simulated.
512 devices in a mesh: dom: 32 (over x, y, core), edge: 16 (over z).
Axes of the slice: x: 4, y: 4, z: 16, core: 2. Of those that a mesh axis runs over, the one named last changes fastest.
Arguments:
- edges: bfloat16 [524288, 512], P(('dom', 'edge')), may hold values from -6 to 6
- atoms: bfloat16 [16384, 256], P(('dom', 'edge')), may hold values from -6 to 6
- reverse: int32 [524288], P(('dom', 'edge')), may hold values from 0 to 524287, as said below
- atom_index: int32 [2, 524288], P(None, ('dom', 'edge')), may hold values from 0 to 511
- tile_source: int32 [8192, 2], P(('dom', 'edge')), may hold values from 0 to 255
- tiles: bfloat16 [8192, 64, 128], P(('dom', 'edge')), may hold values from -1 to 1
- weight_edge: bfloat16 [512, 512], replicated, may hold values from -0.25 to 0.25
- weight_down: bfloat16 [64, 512], replicated, may hold values from -0.25 to 0.25
- weight_up: bfloat16 [2, 64, 512], replicated, may hold values from -0.75 to 0.75
- weight_residual: bfloat16 [1, 2, 512, 512], replicated, may hold values from -0.25 to 0.25
- weight_message: bfloat16 [512, 256], replicated, may hold values from -0.25 to 0.25
- weight_atom: bfloat16 [2, 256, 256], replicated, may hold values from -0.375 to 0.375
- weight_join: bfloat16 [1024, 512], replicated, may hold values from -0.1875 to 0.1875
Outputs:
- new_edges: bfloat16 [524288, 512], P(('dom', 'edge'))
- new_atoms: bfloat16 [16384, 256], P(('dom', 'edge'))
Inputs may be any that keep to these rules, and one draw needn't show every extreme that they name: reverse is an involution without fixed points. The reverse of a row lies on a device of the same edge index. Besides its own partition, the rows of each partition have their reverses in exactly 16 other partitions; at most 32 rows of one device have their reverses in any one other partition, and some device reaches 32.
All inputs are finite; a program needn't handle non-finite values.
Results may differ from a plain program's by a relative error of at most 0.015.
Values may be sent and summed in bfloat16 or wider, within the bound.
A program may use at most 64 MiB of HBM per device.

v0:
```python
import jax
import jax.numpy as jnp
from jax import lax
from jax.sharding import PartitionSpec as P

EPA = 32


root_half = 0.7071067811865476


def product(operand, weights):
    return jnp.dot(operand, weights, preferred_element_type=jnp.float32)


def contract_first(operand, weights):
    return lax.dot_general(
        operand, weights, (((0,), (0,)), ((), ())), preferred_element_type=jnp.float32
    )


def update_atoms(summed, atom_rows, weight_atom):
    scaled = (summed * EPA ** (-0.5)).astype(jnp.bfloat16)
    middle = jax.nn.silu(product(scaled, weight_atom[0])).astype(jnp.bfloat16)
    return (atom_rows.astype(jnp.float32) + product(middle, weight_atom[1])).astype(jnp.bfloat16)


def tile_terms(tile_source, tiles, channels):
    blocks, block_len, tile_width = tiles.shape
    tile_count = tile_width // block_len
    shaped = tiles.reshape(blocks, block_len, tile_count, block_len)
    offsets = jnp.arange(block_len, dtype=jnp.int32)

    def accumulate(running, shard_piece, start_at):
        piece_len = shard_piece.shape[1]
        relative = tile_source * block_len
        columns = relative[:, :, None] + offsets[None, None, :]
        inside = (columns >= 0) & (columns < piece_len)
        picked = jnp.take(shard_piece, jnp.clip(columns, 0, piece_len - 1).reshape(-1), axis=1)
        picked = picked.reshape(channels, blocks, tile_count, block_len)
        picked = jnp.where(inside[None], picked, jnp.zeros((), shard_piece.dtype))
        return jnp.einsum("tbkj,bekj->bte", picked, shaped, preferred_element_type=jnp.float32)

    initial = jnp.zeros((blocks, channels, block_len), jnp.float32)
    return (accumulate, initial)


def body(
    edges,
    atoms,
    reverse,
    atom_index,
    tile_source,
    tiles,
    weight_edge,
    weight_down,
    weight_up,
    weight_residual,
    weight_message,
    weight_atom,
    weight_join,
):
    edge_rows = edges.shape[0]
    channels = weight_down.shape[0]
    domain_count = lax.axis_size("dom")
    shard_count = lax.axis_size("edge")
    own_domain = lax.axis_index("dom")
    capacity = edge_rows // domain_count
    hidden = jax.nn.silu(product(edges, weight_edge)).astype(jnp.bfloat16)
    narrow = jax.nn.silu(
        lax.dot_general(
            weight_down, hidden, (((1,), (1,)), ((), ())), preferred_element_type=jnp.float32
        )
    ).astype(jnp.bfloat16)
    accumulate, initial = tile_terms(tile_source, tiles, channels)
    mixed = accumulate(initial, lax.all_gather(narrow, "edge", axis=1, tiled=True), jnp.int32(0))
    trip_out = mixed.transpose(1, 0, 2).reshape(channels, edge_rows).astype(jnp.bfloat16)
    holder = reverse // (edge_rows * shard_count)
    source_row = reverse % edge_rows
    is_local = holder == own_domain
    positions = jnp.arange(edge_rows, dtype=jnp.int32)
    matching = holder[:, None] == holder[None, :]
    send_slot = jnp.sum(matching & (positions[None, :] < positions[:, None]), axis=1)
    receive_slot = jnp.sum(matching & (source_row[None, :] < source_row[:, None]), axis=1)
    target_slot = jnp.where(is_local, domain_count * capacity, holder * capacity + send_slot)
    send_index = jnp.full((domain_count * capacity,), edge_rows, jnp.int32)
    send_index = send_index.at[target_slot].set(positions, mode="drop")
    filled = send_index < edge_rows
    safe_index = jnp.minimum(send_index, edge_rows - 1)
    fetch_index = jnp.where(is_local, 0, holder * capacity + receive_slot)
    zero_value = jnp.zeros((), jnp.bfloat16)
    swapped = contract_first(trip_out, weight_up[1]).astype(jnp.bfloat16)
    outgoing = jnp.where(filled[:, None], jnp.take(swapped, safe_index, axis=0), zero_value)
    outgoing = outgoing.reshape(domain_count, capacity, swapped.shape[1])
    arrived = lax.all_to_all(outgoing, "dom", split_axis=0, concat_axis=0, tiled=True).reshape(
        domain_count * capacity, swapped.shape[1]
    )
    mirrored = jnp.where(
        is_local[:, None],
        jnp.take(swapped, source_row, axis=0),
        jnp.take(arrived, fetch_index, axis=0),
    )
    direct = contract_first(trip_out, weight_up[0])
    joined = (direct + mirrored.astype(jnp.float32)) * root_half
    edge_state = (edges.astype(jnp.float32) + joined).astype(jnp.bfloat16)
    middle = jax.nn.silu(product(edge_state, weight_residual[0, 0])).astype(jnp.bfloat16)
    branch = jax.nn.silu(product(middle, weight_residual[0, 1]))
    edge_state = ((edge_state.astype(jnp.float32) + branch) * root_half).astype(jnp.bfloat16)
    message = product(edge_state, weight_message).astype(jnp.bfloat16)
    atom_count = atoms.shape[0]
    part_atoms = atom_count * shard_count
    onehot = (atom_index[1][:, None] == jnp.arange(part_atoms, dtype=jnp.int32)[None, :]).astype(
        jnp.bfloat16
    )
    partial_value = contract_first(onehot, message)
    totals = lax.psum(partial_value.astype(jnp.bfloat16), "edge").astype(jnp.float32)
    everyone = lax.all_gather(atoms, "edge", axis=0, tiled=True)
    renewed = update_atoms(totals, everyone, weight_atom)
    own_atoms = lax.dynamic_slice_in_dim(
        renewed, lax.axis_index("edge") * atom_count, atom_count, 0
    )
    gathered = jnp.concatenate(
        [
            jnp.take(renewed, atom_index[0], axis=0),
            jnp.take(renewed, atom_index[1], axis=0),
            edge_state,
        ],
        axis=1,
    )
    update = jax.nn.silu(product(gathered, weight_join))
    new_edges = ((edge_state.astype(jnp.float32) + update) * root_half).astype(jnp.bfloat16)
    return (new_edges, own_atoms)


def solution(mesh):
    placed = (
        P(("dom", "edge"), None),
        P(("dom", "edge"), None),
        P(("dom", "edge")),
        P(None, ("dom", "edge")),
        P(("dom", "edge"), None),
        P(("dom", "edge"), None, None),
        P(),
        P(),
        P(),
        P(),
        P(),
        P(),
        P(),
    )
    return jax.shard_map(
        body,
        mesh=mesh,
        in_specs=placed,
        out_specs=(P(("dom", "edge"), None), P(("dom", "edge"), None)),
        check_vma=False,
    )
```

profile of v0, /device:TPU:24, one launch (start us, length us, event | category | flops | bytes accessed | tf_op | source)
XLA Modules:
  0.0 298.1 jit_solution(15867734499594832848)
XLA Ops:
  7.3 3.4 %multiply_convert_fusion.16 = bf16[64,1024]{1,0:T(8,128)(2,1)} fusion(bf16[64,512]{1,0:T(8,128)(2,1)} %param.24, bf16[1024,512]{1,0:T(8,128)(2,1)} %param.17, bf16[512,512]{1,0:T(8,128)(2,1)} %param.23), kind=kOutput, calls=%fused_computation.57 | convolution fusion | flops 606928896 | bytes 1769472 | tf_op jit(solution)/shard_map/dot_general | solution.py:71
  11.2 2.3 convert_reduce_fusion
  13.6 4.3 %scatter_custom_fusion = s32[1024]{0:T(1024)S(1)} fusion(s32[1024]{0:T(1024)S(1)} %get-tuple-element.15, s32[1024]{0:T(1024)S(1)} %iota.19, s32[]{:T(128)} %constant.97.clone.1), kind=kCustom, calls=%fused_computation.99 | custom fusion | bytes 4100 | tf_op jit(solution)/shard_map/scatter | solution.py:87
  18.1 69.5 %all-gather.2.cloned.1.call-done = bf16[64,16384]{1,0:T(8,128)(2,1)} async-done(((bf16[64,1024]{1,0:T(8,128)(2,1)}), bf16[64,16384]{1,0:T(8,128)(2,1)}) %all-gather.2.cloned.1.call-update) | async-done | bytes 2097168 | tf_op jit(solution)/shard_map/all_gather | solution.py:76
  87.6 4.8 %copy.31 = bf16[64,16384]{0,1:T(8,128)(2,1)} copy(bf16[64,16384]{1,0:T(8,128)(2,1)} %all-gather.2.cloned.1.call-done) | data formatting | bytes 4194304 | tf_op jit(solution)/shard_map/all_gather | solution.py:76
  92.4 8.3 %gather_fusion = bf16[2048,64]{1,0:T(8,128)(2,1)S(1)} fusion(bf16[64,16384]{0,1:T(8,128)(2,1)} %copy.31, s32[2048]{0:T(1024)S(1)} %broadcast_clamp_fusion), kind=kCustom, calls=%fused_computation.5 | custom fusion | bytes 532480 | tf_op jit(solution)/shard_map/jit(_take)/gather | solution.py:39
  101.7 0.5 convolution_convert_fusion
  102.2 4.0 %gather_fusion.2 = bf16[1024,512]{1,0:T(8,128)(2,1)S(1)} fusion(bf16[1024,512]{1,0:T(8,128)(2,1)S(1)} %convolution_convert_fusion, s32[1024]{0:T(1024)S(1)} %fusion.52), kind=kCustom, calls=%fused_computation.2.clone | custom fusion | bytes 2101248 | tf_op jit(solution)/shard_map/jit(_take)/gather | solution.py:93
  106.2 1.6 select_select_fusion.1
  107.8 7.4 %all-to-all-start = ((bf16[32,32,512]{2,1,0:T(8,128)(2,1)}), bf16[32,32,512]{2,1,0:T(8,128)(2,1)S(1)}, u32[]{:S(2)}, u32[]{:S(2)}) async-start(bf16[32,32,512]{2,1,0:T(8,128)(2,1)} %bitcast.54), calls=%async_computation | async-start | bytes 2097152 | tf_op jit(solution)/shard_map/all_to_all | solution.py:95
  115.2 5.1 %gather_fusion.1 = bf16[1024,512]{1,0:T(8,128)(2,1)} fusion(bf16[1024,512]{1,0:T(8,128)(2,1)S(1)} %convolution_convert_fusion, s32[1024]{0:T(1024)S(1)} %fusion.49), kind=kCustom, calls=%fused_computation.clone | custom fusion | bytes 2101248 | tf_op jit(solution)/shard_map/jit(_take)/gather | solution.py:100
  120.3 10.1 %all-to-all-done = bf16[32,32,512]{2,1,0:T(8,128)(2,1)S(1)} async-done(((bf16[32,32,512]{2,1,0:T(8,128)(2,1)}), bf16[32,32,512]{2,1,0:T(8,128)(2,1)S(1)}, u32[]{:S(2)}, u32[]{:S(2)}) %all-to-all-start) | async-done | bytes 1048608 | tf_op jit(solution)/shard_map/all_to_all | solution.py:95
  130.4 5.1 %gather_fusion.3 = bf16[1024,512]{1,0:T(8,128)(2,1)} fusion(bf16[1024,512]{1,0:T(8,128)(2,1)S(1)} %bitcast.53, s32[1024]{0:T(1024)S(1)} %get-tuple-element.14), kind=kCustom, calls=%fused_computation.3.clone | custom fusion | bytes 2101248 | tf_op jit(solution)/shard_map/jit(_take)/gather | solution.py:101
  135.5 3.3 %add_convert_fusion = bf16[1024,512]{1,0:T(8,128)(2,1)} fusion(bf16[1024,512]{1,0:T(8,128)(2,1)} %param.17, bf16[64,1024]{1,0:T(8,128)(2,1)S(1)} %convert_element_type.76, bf16[1024,512]{1,0:T(8,128)(2,1)} %gather_fusion.3, bf16[1024,512]{1,0:T(8,128)(2,1)S(1)} %copy-done.1, pred[1024]{0:T(1024)(128)(4,1)S(1)} %compare_and_fusion.6, ...), kind=kOutput, calls=%fused_computation.22 | convolution fusion | flops 71827456 | bytes 4393984 | tf_op jit(solution)/shard_map/dot_general | solution.py:17
  138.8 4.3 %multiply_convert_fusion.1 = bf16[1024,512]{1,0:T(8,128)(2,1)} fusion(bf16[1024,512]{1,0:T(8,128)(2,1)} %add_convert_fusion, bf16[1,2,512,512]{3,2,1,0:T(8,128)(2,1)S(1)} %copy-done.8), kind=kOutput, calls=%fused_computation.20 | convolution fusion | flops 1080557568 | bytes 4194304 | tf_op jit(solution)/shard_map/dot_general | solution.py:13
  143.2 3.1 %fusion.8 = bf16[512,256]{1,0:T(8,128)(2,1)} fusion(bf16[1024,512]{1,0:T(8,128)(2,1)} %multiply_convert_fusion.1, bf16[512,256]{1,0:T(8,128)(2,1)S(1)} %copy-done.9, s32[1024]{0:T(1024)S(1)} %bitcast.57), kind=kOutput, calls=%fused_computation.30 | convolution fusion | flops 537788416 | bytes 1576960 | tf_op jit(solution)/shard_map/dot_general | solution.py:17
  146.3 30.3 %all_gather.7 = bf16[512,256]{1,0:T(8,128)(2,1)S(1)} all-gather(bf16[32,256]{1,0:T(8,128)(2,1)S(1)} %copy-done.4), channel_id=1, replica_groups=mesh['dom'=32,'edge'=16] {'edge'}, dimensions={0}, use_global_device_ids=true | all-gather | bytes 278528 | tf_op jit(solution)/shard_map/all_gather | solution.py:117
  176.6 101.4 %all-reduce.2.cloned.1.call-done = bf16[512,256]{1,0:T(8,128)(2,1)} async-done(((bf16[512,256]{1,0:T(8,128)(2,1)}), bf16[512,256]{1,0:T(8,128)(2,1)}) %all-reduce.2.cloned.1.call-update) | async-done | bytes 262160 | tf_op jit(solution)/shard_map/psum | solution.py:116
  278.1 1.4 fusion.9
  279.4 3.9 %gather_fusion.4 = bf16[1024,256]{1,0:T(8,128)(2,1)S(1)} fusion(bf16[512,256]{1,0:T(8,128)(2,1)S(1)} %fusion.9, s32[1024]{0:T(1024)S(1)} %fusion.50), kind=kCustom, calls=%fused_computation.1.clone | custom fusion | bytes 1052672 | tf_op jit(solution)/shard_map/jit(_take)/gather | solution.py:124
  283.4 3.9 %gather_fusion.5 = bf16[1024,256]{1,0:T(8,128)(2,1)S(1)} fusion(bf16[512,256]{1,0:T(8,128)(2,1)S(1)} %fusion.9, s32[1024]{0:T(1024)S(1)} %fusion.51), kind=kCustom, calls=%fused_computation.4.clone | custom fusion | bytes 1052672 | tf_op jit(solution)/shard_map/jit(_take)/gather | solution.py:125
  287.3 0.6 constant_dynamic-slice_fusion
  288.0 0.7 broadcast_select_fusion
  288.7 2.6 multiply_convert_fusion
  (52 shorter events, 1.9 us)
Async XLA Ops:
  7.2 281.5 %copy-start = (bf16[1024,512]{1,0:T(8,128)(2,1)S(1)}, bf16[1024,512]{1,0:T(8,128)(2,1)}, u32[]{:S(2)}) copy-start(bf16[1024,512]{1,0:T(8,128)(2,1)} %param.29) | copy-start | bytes 3145732
  7.2 3.5 %copy-start.7 = (s32[16,2]{0,1:T(2,128)S(1)}, s32[16,2]{0,1:T(2,128)}, u32[]{:S(2)}) copy-start(s32[16,2]{0,1:T(2,128)} %param.21) | copy-start | bytes 388
  7.2 3.8 %copy-start.2 = (bf16[16,64,128]{2,1,0:T(8,128)(2,1)S(1)}, bf16[16,64,128]{2,1,0:T(8,128)(2,1)}, u32[]{:S(2)}) copy-start(bf16[16,64,128]{2,1,0:T(8,128)(2,1)} %param.22) | copy-start | bytes 786436
  7.2 4.0 %copy-start.6 = (s32[1024]{0:T(1024)S(1)}, s32[1024]{0:T(1024)}, u32[]{:S(2)}) copy-start(s32[1024]{0:T(1024)} %param.19) | copy-start | bytes 12292
  7.2 10.7 %copy-start.5 = (s32[2,1024]{1,0:T(2,128)S(1)}, s32[2,1024]{1,0:T(2,128)}, u32[]{:S(2)}) copy-start(s32[2,1024]{1,0:T(2,128)} %param.20) | copy-start | bytes 24580
  7.2 80.4 %all-gather.2.cloned.1.call-start = ((), (), s32[]{:S(2)}) async-start(), calls=%async_computation.1 | async-start | bytes 2228224 | tf_op jit(solution)/shard_map/all_gather | solution.py:76
  100.7 1.0 copy-start.3
  107.8 22.7 %all-to-all-start = ((bf16[32,32,512]{2,1,0:T(8,128)(2,1)}), bf16[32,32,512]{2,1,0:T(8,128)(2,1)S(1)}, u32[]{:S(2)}, u32[]{:S(2)}) async-start(bf16[32,32,512]{2,1,0:T(8,128)(2,1)} %bitcast.54), calls=%async_computation | async-start | bytes 2097152 | tf_op jit(solution)/shard_map/all_to_all | solution.py:95
  115.1 162.9 %all-reduce.2.cloned.1.call-start = ((), (), s32[]{:S(2)}) async-start(), calls=%async_computation.2 | async-start | bytes 524288 | tf_op jit(solution)/shard_map/psum | solution.py:116
  130.4 5.1 %copy-start.1 = (bf16[1024,512]{1,0:T(8,128)(2,1)S(1)}, bf16[1024,512]{1,0:T(8,128)(2,1)}, u32[]{:S(2)}) copy-start(bf16[1024,512]{1,0:T(8,128)(2,1)} %gather_fusion.1) | copy-start | bytes 3145732
  135.5 3.3 %copy-start.8 = (bf16[1,2,512,512]{3,2,1,0:T(8,128)(2,1)S(1)}, bf16[1,2,512,512]{3,2,1,0:T(8,128)(2,1)}, u32[]{:S(2)}) copy-start(bf16[1,2,512,512]{3,2,1,0:T(8,128)(2,1)} %param.26) | copy-start | bytes 3145732
  138.8 4.3 %copy-start.9 = (bf16[512,256]{1,0:T(8,128)(2,1)S(1)}, bf16[512,256]{1,0:T(8,128)(2,1)}, u32[]{:S(2)}) copy-start(bf16[512,256]{1,0:T(8,128)(2,1)} %param.27) | copy-start | bytes 786436
  143.2 3.1 %copy-start.4 = (bf16[32,256]{1,0:T(8,128)(2,1)S(1)}, bf16[32,256]{1,0:T(8,128)(2,1)}, u32[]{:S(2)}) copy-start(bf16[32,256]{1,0:T(8,128)(2,1)} %param.18) | copy-start | bytes 49156
  143.2 134.9 %copy-start.10 = (bf16[2,256,256]{2,1,0:T(8,128)(2,1)S(1)}, bf16[2,256,256]{2,1,0:T(8,128)(2,1)}, u32[]{:S(2)}) copy-start(bf16[2,256,256]{2,1,0:T(8,128)(2,1)} %param.28) | copy-start | bytes 786436
  287.3 1.4 copy-start.11
Sparse Core Ops, SparseCore 0:
  10.8 76.7 all-gather.1
  146.4 131.5 all-reduce.1
where the time goes:
time: 299 us; the launch traced here: 298 us
  waiting for transfers between devices  181 us (61%)
  local copies, waits for them, and re-layouts  41.2 us (14%)
  blocking collectives  30.3 us (10%)
  matrix products  18.8 us (6%)
  between operations  14.4 us (5%)
  starting transfers between devices  7.44 us (2%)
  other arithmetic  4.9 us (2%)
    psum x1, waiting for transfers between devices, body(): lax.psum(partial_value.astype(jnp.bfloat16), 'edge').astype(jnp.float32)  101 us
    all_gather x1, waiting for transfers between devices, body(): lax.all_gather(narrow, 'edge', axis=1, tiled=True)  69.5 us
    all_gather x1, blocking collectives, body(): everyone = lax.all_gather(atoms, 'edge', axis=0, tiled=True)  30.3 us
    all_to_all x1, waiting for transfers between devices, body(): lax.all_to_all(outgoing, 'dom', split_axis=0, concat_axis=0, tiled=True)  10.1 us
    gather x2, local copies, waits for them, and re-layouts, accumulate(): jnp.take(shard_piece, jnp.clip(columns, 0, piece_len - 1).reshape(-1), ax...  8.58 us
    dot_general x3, matrix products, product(): return jnp.dot(operand, weights, preferred_element_type=jnp.float32)  8.24 us
    all_to_all x1, starting transfers between devices, body(): lax.all_to_all(outgoing, 'dom', split_axis=0, concat_axis=0, tiled=True)  7.36 us
    dot_general x3, matrix products, contract_first(): lax.dot_general(operand, weights, (((0,), (0,)), ((), ())), preferred_ele...  6.92 us
  transfers between devices with their start and end apart: 3, of which 3 were waited for; matrix products, arithmetic and copies ran while one was open for 4% of the time, Pallas kernels for 0%

commit v1 on v0

v1 whole, which is shorter than its diff:
```python
import functools

import jax
import jax.numpy as jnp
from jax import lax
from jax.experimental import pallas as pl
from jax.experimental.pallas import tpu as pltpu
from jax.sharding import PartitionSpec as P

EPA = 32
ROOT_HALF = 0.7071067811865476
MESH = pl.DeviceIdType.MESH
BF16 = jnp.bfloat16
F32 = jnp.float32
I32 = jnp.int32
CHUNKS = 4
PIECES = 8


def silu(v):
    half = 0.5 * v
    return half + half * jnp.tanh(half)


def dot(a, b):
    return jnp.dot(a, b, preferred_element_type=F32)


def dot_nt(a, b):
    return lax.dot_general(a, b, (((1,), (1,)), ((), ())), preferred_element_type=F32)


def iota(shape, axis):
    return lax.broadcasted_iota(I32, shape, axis)


def log2(n):
    assert n & (n - 1) == 0
    return n.bit_length() - 1


def flag(cond):
    return jnp.where(cond, jnp.float32(1), jnp.float32(0))


def kernel(
    n_dom,
    n_edge,
    ts_ref,
    rev_ref,
    ai_ref,
    atoms_ref,
    wd_ref,
    edges_h,
    tiles_h,
    we_h,
    wup_h,
    wres_h,
    wmsg_h,
    watom_h,
    wjoin_h,
    out_ref,
    natoms_ref,
    edges_v,
    tiles_v,
    we_v,
    wup_v,
    wres_v,
    wmsg_v,
    watom_v,
    wjoin_v,
    gath,
    trip_v,
    pack_v,
    arr_v,
    mir_v,
    sel_v,
    loc_v,
    rec_v,
    keep_v,
    tgt_t,
    src_g,
    tgt_g,
    cols_v,
    rank_v,
    es_v,
    msg_v,
    pre_v,
    rs_v,
    rr_v,
    na_v,
    load_sem,
    ring_send,
    ring_recv,
    x_sem,
    z_sem,
):
    me_d = lax.axis_index("dom")
    me_z = lax.axis_index("edge")
    rows, width = edges_v.shape
    groups = gath.shape[0] // n_edge
    part_atoms, atom_width = rs_v.shape
    own_atoms = part_atoms // n_edge
    half_cap = pack_v.shape[0] // n_dom
    slots = pack_v.shape[0]
    steps = n_edge // 2
    per = groups // CHUNKS
    edge_half = rows // 2
    sub = edge_half // CHUNKS
    right = lax.rem(me_z + 1, n_edge)
    left = lax.rem(me_z + n_edge - 1, n_edge)

    def load(i, src, dst):
        return pltpu.make_async_copy(src, dst, load_sem.at[i])

    edge_loads = [
        [
            load(2 * c + h, edges_h.at[pl.ds(h * edge_half + c * sub, sub)], edges_v.at[pl.ds(h * edge_half + c * sub, sub)])
            for h in range(2)
        ]
        for c in range(CHUNKS)
    ]
    base = 2 * CHUNKS
    we_load = load(base, we_h, we_v)
    others = [
        load(base + 1, tiles_h, tiles_v),
        load(base + 2, wup_h, wup_v),
        load(base + 3, wres_h, wres_v),
        load(base + 4, wmsg_h, wmsg_v),
        load(base + 5, watom_h, watom_v),
        load(base + 6, wjoin_h, wjoin_v),
    ]
    we_load.start()
    for pair in edge_loads:
        for one in pair:
            one.start()

    barrier = pltpu.get_barrier_semaphore()
    for peer in (left, right):
        pl.semaphore_signal(barrier, inc=1, device_id={"edge": peer}, device_id_type=MESH)

    def greet(k, carry):
        pl.semaphore_signal(
            barrier, inc=1, device_id={"dom": lax.rem(me_d + k, n_dom)}, device_id_type=MESH
        )
        return carry

    lax.fori_loop(1, n_dom, greet, 0)
    for one in others:
        one.start()

    def ring(direction, s, c, receiving):
        if direction == 0:
            slot = lax.rem(me_z - s - (1 if receiving else 0) + 2 * n_edge, n_edge)
            to = right
        else:
            slot = lax.rem(me_z + s + (1 if receiving else 0), n_edge)
            to = left
        view = gath.at[pl.ds(slot * groups + c * per, per)]
        return pltpu.make_async_remote_copy(
            src_ref=view,
            dst_ref=view,
            send_sem=ring_send.at[direction, s, c],
            recv_sem=ring_recv.at[direction, s, c],
            device_id={"edge": to},
            device_id_type=MESH,
        )

    zeros_down = jnp.zeros_like(wd_ref[...])
    wd_lo = jnp.concatenate([wd_ref[...], zeros_down], axis=0)
    wd_hi = jnp.concatenate([zeros_down, wd_ref[...]], axis=0)
    we_load.wait()
    for c in range(CHUNKS):
        for one in edge_loads[c]:
            one.wait()
        x = jnp.concatenate(
            [edges_v[pl.ds(c * sub, sub)], edges_v[pl.ds(edge_half + c * sub, sub)]], axis=0
        )
        hidden = silu(dot(x, we_v[...])).astype(BF16)
        narrow = silu(dot_nt(hidden[:sub], wd_lo) + dot_nt(hidden[sub:], wd_hi)).astype(BF16)
        gath[pl.ds(me_z * groups + c * per, per)] = narrow.reshape(per, narrow.shape[0] // per, narrow.shape[1])
        if c == 0:
            pl.semaphore_wait(barrier, n_dom + 1)
        ring(0, 0, c, False).start()
        ring(1, 0, c, False).start()

    shift = log2(rows * n_edge)
    rev_row = rev_ref[...]
    hold_row = lax.shift_right_logical(rev_row, shift)
    local_row = hold_row == me_d
    src_row = rev_row & (rows - 1)
    for i, row in enumerate((rev_row, ai_ref[0:1], ai_ref[1:2])):
        cols_v[i] = jnp.transpose(jnp.broadcast_to(row.astype(F32), (8, rows))).astype(I32)
    piece = rows // PIECES

    def forward(t):
        s, c = 1 + lax.div(t, CHUNKS), lax.rem(t, CHUNKS)
        for direction in range(2):
            ring(direction, s - 1, c, True).wait_recv()
            ring(direction, s, c, False).start()

    def ranks(i):
        at = i * piece
        here = pl.ds(at, piece)
        rev_col = cols_v[0, here, 0:1]
        hold_col = lax.shift_right_logical(rev_col, shift)
        before = (hold_col == hold_row) & (iota((piece, rows), 0) + at < iota((piece, rows), 1))
        rank_v[...] = rank_v[...] + jnp.sum(flag(before), axis=0, keepdims=True)
        lower = (rev_row >= lax.shift_left(hold_col, shift)) & (rev_row < rev_col)
        rank = jnp.sum(flag(lower), axis=1, keepdims=True).astype(I32)
        high = jnp.where(rank >= half_cap, 1, 0)
        code = jnp.where(hold_col == me_d, -1, hold_col * half_cap + rank - high * half_cap)
        rec_v[here] = flag(iota((piece, slots), 1) == code).astype(BF16)
        keep_v[here] = flag((iota((piece, 128), 1) >= 64) == (high == 1))

    def select(i):
        at = i * piece
        here = pl.ds(at, piece)
        rank = rank_v[0:1].astype(I32)
        high = jnp.where(rank >= half_cap, 1, 0)
        code = jnp.where(local_row, -1, hold_row * half_cap + rank + high * (slots - half_cap))
        at_slot = i * (2 * slots // PIECES)
        sel_v[pl.ds(at_slot, 2 * slots // PIECES)] = flag(
            iota((2 * slots // PIECES, rows), 0) + at_slot == code
        ).astype(BF16)
        rev_col = cols_v[0, here, 0:1]
        from_col = jnp.where(
            lax.shift_right_logical(rev_col, shift) == me_d, rev_col & (rows - 1), -1
        )
        loc_v[here] = flag(iota((piece, rows), 1) == from_col).astype(BF16)

    def onehots(i):
        here = pl.ds(i * piece, piece)
        atom_piece = part_atoms // PIECES
        tgt_t[pl.ds(i * atom_piece, atom_piece)] = flag(
            iota((atom_piece, rows), 0) + i * atom_piece == ai_ref[1:2]
        ).astype(BF16)
        lanes = iota((piece, part_atoms), 1)
        src_g[here] = flag(lanes == cols_v[1, here, 0:1]).astype(BF16)
        tgt_g[here] = flag(lanes == cols_v[2, here, 0:1]).astype(BF16)

    rank_v[...] = jnp.zeros_like(rank_v)
    middle = (steps - 2) * CHUNKS
    for k, work in enumerate((ranks, select, onehots)):

        def turn(i, carry, k=k, work=work):
            if k * PIECES < middle:
                forward(k * PIECES + i)
            work(i)
            return carry

        lax.fori_loop(0, PIECES, turn, 0)

    arr_v[pl.ds(me_d * half_cap, half_cap)] = jnp.zeros((half_cap, 128), BF16)

    last = steps - 1
    split = CHUNKS // 2
    for c in range(CHUNKS):
        for direction in range(2):
            ring(direction, last - 1, c, True).wait_recv()
            if (c < split) == (direction == 0):
                ring(direction, last, c, False).start()
    for c in range(CHUNKS):
        ring(0 if c < split else 1, last, c, True).wait_recv()

    others[0].wait()
    blocks = tiles_v.shape[0]
    lane_half = lax.shift_right_logical(iota((64, 128), 1), 6)
    for b in range(blocks):
        picked = []
        for k in range(2):
            source = ts_ref[b, k]
            owner = lax.shift_right_logical(source, log2(blocks))
            inner = source & (blocks - 1)
            value = gath[owner * groups + (inner & (groups - 1))]
            picked.append(
                jnp.where(lane_half == lax.shift_right_logical(inner, log2(groups)), value, jnp.zeros_like(value))
            )
        mixed = dot(tiles_v[b], jnp.concatenate(picked, axis=0))
        trip_v[pl.ds(b * 64, 64)] = (mixed + pltpu.roll(mixed, 64, 1)).astype(BF16)

    low_lanes = iota((slots, 128), 1) < 64
    pack_v[...] = jnp.where(
        low_lanes, dot(sel_v[pl.ds(0, slots)], trip_v[...]), dot(sel_v[pl.ds(slots, slots)], trip_v[...])
    ).astype(BF16)

    def send_dom(k, carry):
        peer = lax.rem(me_d + k, n_dom)
        pltpu.make_async_remote_copy(
            src_ref=pack_v.at[pl.ds(peer * half_cap, half_cap)],
            dst_ref=arr_v.at[pl.ds(me_d * half_cap, half_cap)],
            send_sem=x_sem.at[0],
            recv_sem=x_sem.at[1],
            device_id={"dom": peer},
            device_id_type=MESH,
        ).start()
        return carry

    lax.fori_loop(1, n_dom, send_dom, 0)
    all_but_one = pl.ds(0, slots - half_cap)
    exchange = pltpu.make_async_remote_copy(
        src_ref=pack_v.at[all_but_one],
        dst_ref=arr_v.at[all_but_one],
        send_sem=x_sem.at[0],
        recv_sem=x_sem.at[1],
        device_id={"dom": lax.rem(me_d + 1, n_dom)},
        device_id_type=MESH,
    )
    part = rows // 4
    for i in range(4):
        mir_v[pl.ds(i * part, part)] = dot(loc_v[pl.ds(i * part, part)], trip_v[...])
    for one in others[1:]:
        one.wait()
    exchange.wait()

    def edge_part(i, carry):
        here = pl.ds(i * part, part)
        found = dot(rec_v[here], arr_v[...]) * keep_v[here]
        mirrored = (found + pltpu.roll(found, 64, 1) + mir_v[here]).astype(BF16)
        both = jnp.where(iota((part, 128), 1) < 64, trip_v[here], mirrored)
        state = (edges_v[here].astype(F32) + dot(both, wup_v[...]) * ROOT_HALF).astype(BF16)
        middle = silu(dot(state, wres_v[0])).astype(BF16)
        branch = silu(dot(middle, wres_v[1]))
        state = ((state.astype(F32) + branch) * ROOT_HALF).astype(BF16)
        es_v[here] = state
        msg_v[here] = dot(state, wmsg_v[...]).astype(BF16)
        return carry

    lax.fori_loop(0, 4, edge_part, 0)

    a_part = part_atoms // 4
    for i in range(4):
        here = pl.ds(i * a_part, a_part)
        rs_v[here] = dot(tgt_t[here], msg_v[...]).astype(BF16)

    def send_sums(k, carry):
        peer = lax.rem(me_z + k, n_edge)
        pltpu.make_async_remote_copy(
            src_ref=rs_v.at[pl.ds(peer * own_atoms, own_atoms)],
            dst_ref=rr_v.at[pl.ds(me_z * own_atoms, own_atoms)],
            send_sem=z_sem.at[0],
            recv_sem=z_sem.at[1],
            device_id={"edge": peer},
            device_id_type=MESH,
        ).start()
        return carry

    lax.fori_loop(1, n_edge, send_sums, 0)
    own = pl.ds(me_z * own_atoms, own_atoms)
    rr_v[own] = rs_v[own]

    def pre_part(i, carry):
        here = pl.ds(i * part, part)
        pre_v[here] = dot(es_v[here], wjoin_v[pl.ds(2 * atom_width, width)])
        return carry

    lax.fori_loop(0, 4, pre_part, 0)
    most = pl.ds(0, part_atoms - own_atoms)
    sums = pltpu.make_async_remote_copy(
        src_ref=rs_v.at[most],
        dst_ref=rr_v.at[most],
        send_sem=z_sem.at[0],
        recv_sem=z_sem.at[1],
        device_id={"edge": right},
        device_id_type=MESH,
    )
    sums.wait()
    total = jnp.zeros((own_atoms, atom_width), F32)
    for j in range(n_edge):
        total = total + rr_v[pl.ds(j * own_atoms, own_atoms)].astype(F32)
    scaled = (total * EPA ** (-0.5)).astype(BF16)
    middle_atoms = silu(dot(scaled, watom_v[0])).astype(BF16)
    fresh = (atoms_ref[...].astype(F32) + dot(middle_atoms, watom_v[1])).astype(BF16)
    natoms_ref[...] = fresh
    na_v[own] = fresh

    def send_atoms(k, carry):
        peer = lax.rem(me_z + k, n_edge)
        pltpu.make_async_remote_copy(
            src_ref=na_v.at[own],
            dst_ref=na_v.at[own],
            send_sem=z_sem.at[2],
            recv_sem=z_sem.at[3],
            device_id={"edge": peer},
            device_id_type=MESH,
        ).start()
        return carry

    lax.fori_loop(1, n_edge, send_atoms, 0)
    pltpu.make_async_remote_copy(
        src_ref=na_v.at[most],
        dst_ref=na_v.at[most],
        send_sem=z_sem.at[2],
        recv_sem=z_sem.at[3],
        device_id={"edge": right},
        device_id_type=MESH,
    ).wait()

    def final_part(i, carry):
        here = pl.ds(i * part, part)
        ends = jnp.concatenate([dot(src_g[here], na_v[...]), dot(tgt_g[here], na_v[...])], axis=1).astype(BF16)
        update = silu(dot(ends, wjoin_v[pl.ds(0, 2 * atom_width)]) + pre_v[here])
        out_ref[here] = ((es_v[here].astype(F32) + update) * ROOT_HALF).astype(BF16)
        return carry

    lax.fori_loop(0, 4, final_part, 0)

    def drain(t, carry):
        s, c = lax.div(t, CHUNKS), lax.rem(t, CHUNKS)
        for direction in range(2):
            ring(direction, s, c, False).wait_send()
        return carry

    lax.fori_loop(0, last * CHUNKS, drain, 0)
    for c in range(CHUNKS):
        ring(0 if c < split else 1, last, c, False).wait_send()


def body(n_dom, n_edge, edges, atoms, reverse, atom_index, tile_source, tiles, weight_edge, weight_down, weight_up,
         weight_residual, weight_message, weight_atom, weight_join):
    rows, width = edges.shape
    own_atoms, atom_width = atoms.shape
    part_atoms = own_atoms * n_edge
    blocks = tiles.shape[0]
    channels = weight_down.shape[0]
    assert channels == 64 and tiles.shape[1:] == (64, 128)
    groups = blocks // 2
    capacity = rows // n_dom
    slots = n_dom * capacity // 2
    vmem = pl.BlockSpec(memory_space=pltpu.VMEM)
    hbm = pl.BlockSpec(memory_space=pl.ANY)
    return pl.pallas_call(
        functools.partial(kernel, n_dom, n_edge),
        out_shape=(
            jax.ShapeDtypeStruct((rows, width), BF16),
            jax.ShapeDtypeStruct((own_atoms, atom_width), BF16),
        ),
        in_specs=[pl.BlockSpec(memory_space=pltpu.SMEM)] + [vmem] * 4 + [hbm] * 8,
        out_specs=(vmem, vmem),
        scratch_shapes=[
            pltpu.VMEM((rows, width), BF16),
            pltpu.VMEM(tiles.shape, BF16),
            pltpu.VMEM(weight_edge.shape, BF16),
            pltpu.VMEM((2 * channels, width), BF16),
            pltpu.VMEM((2, width, width), BF16),
            pltpu.VMEM(weight_message.shape, BF16),
            pltpu.VMEM(weight_atom.shape, BF16),
            pltpu.VMEM(weight_join.shape, BF16),
            pltpu.VMEM((n_edge * groups, 64, 128), BF16),
            pltpu.VMEM((rows, 128), BF16),
            pltpu.VMEM((slots, 128), BF16),
            pltpu.VMEM((slots, 128), BF16),
            pltpu.VMEM((rows, 128), F32),
            pltpu.VMEM((2 * slots, rows), BF16),
            pltpu.VMEM((rows, rows), BF16),
            pltpu.VMEM((rows, slots), BF16),
            pltpu.VMEM((rows, 128), F32),
            pltpu.VMEM((part_atoms, rows), BF16),
            pltpu.VMEM((rows, part_atoms), BF16),
            pltpu.VMEM((rows, part_atoms), BF16),
            pltpu.VMEM((3, rows, 8), I32),
            pltpu.VMEM((8, rows), F32),
            pltpu.VMEM((rows, width), BF16),
            pltpu.VMEM((rows, atom_width), BF16),
            pltpu.VMEM((rows, width), F32),
            pltpu.VMEM((part_atoms, atom_width), BF16),
            pltpu.VMEM((part_atoms, atom_width), BF16),
            pltpu.VMEM((part_atoms, atom_width), BF16),
            pltpu.SemaphoreType.DMA((2 * CHUNKS + 7,)),
            pltpu.SemaphoreType.DMA((2, n_edge // 2, CHUNKS)),
            pltpu.SemaphoreType.DMA((2, n_edge // 2, CHUNKS)),
            pltpu.SemaphoreType.DMA((2,)),
            pltpu.SemaphoreType.DMA((4,)),
        ],
        compiler_params=pltpu.CompilerParams(
            collective_id=0, has_side_effects=True, vmem_limit_bytes=56 * 1024 * 1024
        ),
    )(
        tile_source,
        reverse.reshape(1, rows),
        atom_index,
        atoms,
        weight_down,
        edges,
        tiles,
        weight_edge,
        weight_up.reshape(2 * channels, width),
        weight_residual.reshape(2, width, width),
        weight_message,
        weight_atom,
        weight_join,
    )


def solution(mesh):
    n_dom, n_edge = mesh.shape["dom"], mesh.shape["edge"]
    placed = (
        P(("dom", "edge"), None),
        P(("dom", "edge"), None),
        P(("dom", "edge")),
        P(None, ("dom", "edge")),
        P(("dom", "edge"), None),
        P(("dom", "edge"), None, None),
        P(),
        P(),
        P(),
        P(),
        P(),
        P(),
        P(),
    )
    return jax.shard_map(
        functools.partial(body, n_dom, n_edge),
        mesh=mesh,
        in_specs=placed,
        out_specs=(P(("dom", "edge"), None), P(("dom", "edge"), None)),
        check_vma=False,
    )
```

time: 299 us -> 94.2 us (0.32)
  waiting for transfers between devices: 181 us -> 0 us
  Pallas kernels: 0 us -> 88.2 us
  local copies, waits for them, and re-layouts: 41.2 us -> 4.23 us
  blocking collectives: 30.3 us -> 0 us
  matrix products: 18.8 us -> 0 us
  between operations: 14.4 us -> 0.66 us
  starting transfers between devices: 7.44 us -> 0 us
  other arithmetic: 4.9 us -> 0 us
    psum x1 -> x0, waiting for transfers between devices: 101 us -> none  [body(): lax.psum(partial_value.astype(jnp.bfloat16), 'edge').astype(jnp.float32)]
    pallas_call x0 -> x1, Pallas kernels: none -> 88.2 us  [body(): pl.pallas_call(functools.partial(kernel, n_dom, n_edge), out_shape=(jax.S...]
    all_gather x1 -> x0, waiting for transfers between devices: 69.5 us -> none  [body(): lax.all_gather(narrow, 'edge', axis=1, tiled=True)]
    gather x7 -> x0, local copies, waits for them, and re-layouts: 30.6 us -> none  [the longest x2 8.58 us: accumulate(): jnp.take(shard_piece, jnp.clip(columns, 0, piece_len - 1).reshape(-1), ax...]
    all_gather x1 -> x0, blocking collectives: 30.3 us -> none  [body(): everyone = lax.all_gather(atoms, 'edge', axis=0, tiled=True)]
    dot_general x8 -> x0, matrix products: 18.8 us -> none  [the longest x3 8.24 us: product(): return jnp.dot(operand, weights, preferred_element_type=jnp.float32)]
    all_to_all x1 -> x0, waiting for transfers between devices: 10.1 us -> none  [body(): lax.all_to_all(outgoing, 'dom', split_axis=0, concat_axis=0, tiled=True)]
    all_to_all x1 -> x0, starting transfers between devices: 7.36 us -> none  [body(): lax.all_to_all(outgoing, 'dom', split_axis=0, concat_axis=0, tiled=True)]
  transfers between devices with their start and end apart: 3 -> 0, of which waited for: 3 -> 0; matrix products, arithmetic and copies ran while one was open for 4% -> 0% of each run, Pallas kernels for 0% -> 0%
where the time goes in v1:
time: 94.2 us; the launch traced here: 93.1 us
  Pallas kernels  88.2 us (94%)
  local copies, waits for them, and re-layouts  4.23 us (4%)
    pallas_call x1, Pallas kernels, body(): pl.pallas_call(functools.partial(kernel, n_dom, n_edge), out_shape=(jax.S...  88.2 us
    unnamed x7, local copies, waits for them, and re-layouts  4.23 us

profile of v1, /device:TPU:24, one launch (start us, length us, event | category | flops | bytes accessed | tf_op | source)
XLA Modules:
  0.0 93.1 jit_solution(3374353948696629101)
XLA Ops:
  0.6 0.0 copy-start.1
  0.6 0.7 copy-done.1
  1.3 0.7 copy.15.ts_ref
  2.0 88.2 %shard_map.140 = (bf16[1024,512]{1,0:T(8,128)(2,1)}, bf16[32,256]{1,0:T(8,128)(2,1)}) custom-call(s32[16,2]{1,0:T(8,128)} %copy.15.ts_ref, s32[1,1024]{1,0:T(1,128)} %bitcast.5, s32[2,1024]{1,0:T(2,128)} %ai_ref.1, bf16[32,256]{1,0:T(8,128)(2,1)} %atoms_ref.1, bf16[64,512]{1,0:T(8,128)(2,1)} %wd_ref.1, bf16[1024,512]{1,0:T(8,128)(2,1)} %edges_h.1, ...), custom_call_target="tpu_custom_call" | custom-call | tf_op jit(solution)/shard_map/pallas_call | solution.py:432
  90.2 0.0 copy-start
  90.2 2.3 %copy.18 = bf16[1024,512]{1,0:T(8,128)(2,1)} copy(bf16[1024,512]{1,0:T(8,128)(2,1)} %get-tuple-element.4) | data formatting | bytes 2097152
  92.5 0.0 copy-done
  92.5 0.6 copy.19
Async XLA Ops:
  0.6 0.7 copy-start.1
  90.2 2.3 %copy-start = (bf16[32,256]{1,0:T(8,128)(2,1)S(1)}, bf16[32,256]{1,0:T(8,128)(2,1)}, u32[]{:S(2)}) copy-start(bf16[32,256]{1,0:T(8,128)(2,1)} %get-tuple-element.5) | copy-start | bytes 49156

commit v2 on v1

--- a/solution.py
+++ b/solution.py
@@ -13,8 +13,8 @@
 BF16 = jnp.bfloat16
 F32 = jnp.float32
 I32 = jnp.int32
-CHUNKS = 4
-PIECES = 8
+CHUNKS = 8
+PIECES = 16
 
 
 def silu(v):
@@ -87,7 +87,9 @@
     msg_v,
     pre_v,
     rs_v,
-    rr_v,
+    rel_v,
+    hop_v,
+    fin_v,
     na_v,
     load_sem,
     ring_send,
@@ -269,7 +271,7 @@
     for b in range(blocks):
         picked = []
         for k in range(2):
-            source = ts_ref[b, k]
+            source = ts_ref[k, b]
             owner = lax.shift_right_logical(source, log2(blocks))
             inner = source & (blocks - 1)
             value = gath[owner * groups + (inner & (groups - 1))]
@@ -326,75 +328,87 @@
         msg_v[here] = dot(state, wmsg_v[...]).astype(BF16)
         return carry
 
-    lax.fori_loop(0, 4, edge_part, 0)
+    for i in range(4):
+        edge_part(i, 0)
 
     a_part = part_atoms // 4
     for i in range(4):
         here = pl.ds(i * a_part, a_part)
         rs_v[here] = dot(tgt_t[here], msg_v[...]).astype(BF16)
 
-    def send_sums(k, carry):
-        peer = lax.rem(me_z + k, n_edge)
+    def push(src, dst, sems, peer):
         pltpu.make_async_remote_copy(
-            src_ref=rs_v.at[pl.ds(peer * own_atoms, own_atoms)],
-            dst_ref=rr_v.at[pl.ds(me_z * own_atoms, own_atoms)],
-            send_sem=z_sem.at[0],
-            recv_sem=z_sem.at[1],
+            src_ref=src,
+            dst_ref=dst,
+            send_sem=z_sem.at[sems[0]],
+            recv_sem=z_sem.at[sems[1]],
             device_id={"edge": peer},
             device_id_type=MESH,
         ).start()
-        return carry
-
-    lax.fori_loop(1, n_edge, send_sums, 0)
-    own = pl.ds(me_z * own_atoms, own_atoms)
-    rr_v[own] = rs_v[own]
+
+    def local(ref, sems):
+        return pltpu.make_async_remote_copy(
+            src_ref=ref,
+            dst_ref=ref,
+            send_sem=z_sem.at[sems[0]],
+            recv_sem=z_sem.at[sems[1]],
+            device_id={"edge": right},
+            device_id_type=MESH,
+        )
+
+    def away(d):
+        return lax.rem(me_z + d + n_edge, n_edge)
+
+    def atoms_of(device):
+        return pl.ds(device * own_atoms, own_atoms)
+
+    def slot_of(i):
+        return pl.ds(i * own_atoms, own_atoms)
+
+    hop = n_edge // 4
+    for d in range(2 * hop, hop, -1):
+        push(rs_v.at[atoms_of(away(d))], rel_v.at[slot_of(d - hop - 1)], (0, 1), away(d - hop))
+        if d < 2 * hop:
+            push(rs_v.at[atoms_of(away(-d))], rel_v.at[slot_of(d - 1)], (0, 1), away(hop - d))
+    for d in range(hop - 1, 0, -1):
+        push(rs_v.at[atoms_of(away(d))], fin_v.at[slot_of(d - 1)], (0, 2), away(d))
+        push(rs_v.at[atoms_of(away(-d))], fin_v.at[slot_of(hop + d - 1)], (0, 2), away(-d))
 
     def pre_part(i, carry):
         here = pl.ds(i * part, part)
         pre_v[here] = dot(es_v[here], wjoin_v[pl.ds(2 * atom_width, width)])
         return carry
 
+    local(rel_v, (0, 1)).wait_recv()
+    for side, first, count in ((0, 0, hop), (1, hop, hop - 1)):
+        owner = away(hop if side == 0 else -hop)
+        relayed = rs_v[atoms_of(owner)].astype(F32)
+        for i in range(first, first + count):
+            relayed = relayed + rel_v[slot_of(i)].astype(F32)
+        hop_v[slot_of(side)] = relayed.astype(BF16)
+        push(hop_v.at[slot_of(side)], fin_v.at[slot_of((side + 1) * hop - 1)], (0, 2), owner)
     lax.fori_loop(0, 4, pre_part, 0)
-    most = pl.ds(0, part_atoms - own_atoms)
-    sums = pltpu.make_async_remote_copy(
-        src_ref=rs_v.at[most],
-        dst_ref=rr_v.at[most],
-        send_sem=z_sem.at[0],
-        recv_sem=z_sem.at[1],
-        device_id={"edge": right},
-        device_id_type=MESH,
-    )
-    sums.wait()
-    total = jnp.zeros((own_atoms, atom_width), F32)
-    for j in range(n_edge):
-        total = total + rr_v[pl.ds(j * own_atoms, own_atoms)].astype(F32)
+    local(fin_v, (0, 2)).wait_recv()
+    own = atoms_of(me_z)
+    total = rs_v[own].astype(F32)
+    for i in range(2 * hop):
+        total = total + fin_v[slot_of(i)].astype(F32)
     scaled = (total * EPA ** (-0.5)).astype(BF16)
     middle_atoms = silu(dot(scaled, watom_v[0])).astype(BF16)
     fresh = (atoms_ref[...].astype(F32) + dot(middle_atoms, watom_v[1])).astype(BF16)
     natoms_ref[...] = fresh
     na_v[own] = fresh
 
-    def send_atoms(k, carry):
-        peer = lax.rem(me_z + k, n_edge)
-        pltpu.make_async_remote_copy(
-            src_ref=na_v.at[own],
-            dst_ref=na_v.at[own],
-            send_sem=z_sem.at[2],
-            recv_sem=z_sem.at[3],
-            device_id={"edge": peer},
-            device_id_type=MESH,
-        ).start()
-        return carry
-
-    lax.fori_loop(1, n_edge, send_atoms, 0)
-    pltpu.make_async_remote_copy(
-        src_ref=na_v.at[most],
-        dst_ref=na_v.at[most],
-        send_sem=z_sem.at[2],
-        recv_sem=z_sem.at[3],
-        device_id={"edge": right},
-        device_id_type=MESH,
-    ).wait()
+    for d in range(hop, 0, -1):
+        push(na_v.at[own], na_v.at[own], (3, 4 if d == hop else 6), away(d))
+        push(na_v.at[own], na_v.at[own], (3, 5 if d == hop else 6), away(-d))
+    for side in range(2):
+        sign = 1 - 2 * side
+        passed = na_v.at[atoms_of(away(-sign * hop))]
+        local(passed, (3, 4 + side)).wait_recv()
+        for d in range(hop - side, 0, -1):
+            push(passed, passed, (3, 6), away(sign * d))
+    local(na_v.at[pl.ds(0, (n_edge - 3) * own_atoms)], (3, 6)).wait_recv()
 
     def final_part(i, carry):
         here = pl.ds(i * part, part)
@@ -403,8 +417,12 @@
         out_ref[here] = ((es_v[here].astype(F32) + update) * ROOT_HALF).astype(BF16)
         return carry
 
-    lax.fori_loop(0, 4, final_part, 0)
-
+    for i in range(4):
+        final_part(i, 0)
+
+    most = pl.ds(0, part_atoms - own_atoms)
+    local(rs_v.at[most], (0, 1)).wait_send()
+    local(na_v.at[most], (3, 4)).wait_send()
     def drain(t, carry):
         s, c = lax.div(t, CHUNKS), lax.rem(t, CHUNKS)
         for direction in range(2):
@@ -464,19 +482,21 @@
             pltpu.VMEM((rows, atom_width), BF16),
             pltpu.VMEM((rows, width), F32),
             pltpu.VMEM((part_atoms, atom_width), BF16),
-            pltpu.VMEM((part_atoms, atom_width), BF16),
+            pltpu.VMEM((part_atoms // 2 - own_atoms, atom_width), BF16),
+            pltpu.VMEM((2 * own_atoms, atom_width), BF16),
+            pltpu.VMEM((part_atoms // 2, atom_width), BF16),
             pltpu.VMEM((part_atoms, atom_width), BF16),
             pltpu.SemaphoreType.DMA((2 * CHUNKS + 7,)),
             pltpu.SemaphoreType.DMA((2, n_edge // 2, CHUNKS)),
             pltpu.SemaphoreType.DMA((2, n_edge // 2, CHUNKS)),
             pltpu.SemaphoreType.DMA((2,)),
-            pltpu.SemaphoreType.DMA((4,)),
+            pltpu.SemaphoreType.DMA((7,)),
         ],
         compiler_params=pltpu.CompilerParams(
             collective_id=0, has_side_effects=True, vmem_limit_bytes=56 * 1024 * 1024
         ),
     )(
-        tile_source,
+        tile_source.T,
         reverse.reshape(1, rows),
         atom_index,
         atoms,

time: 94.2 us -> 85.3 us (0.906)
  Pallas kernels: 88.2 us -> 81.6 us
  local copies, waits for them, and re-layouts: 4.23 us -> 2.88 us
    pallas_call x1, Pallas kernels: 88.2 us -> 81.6 us  [body(): pl.pallas_call(functools.partial(kernel, n_dom, n_edge), out_shape=(jax.S...]
    unnamed x7 -> x4, local copies, waits for them, and re-layouts: 4.23 us -> 2.88 us
where the time goes in v2:
time: 85.3 us; the launch traced here: 85.1 us
  Pallas kernels  81.6 us (96%)
  local copies, waits for them, and re-layouts  2.88 us (3%)
    pallas_call x1, Pallas kernels, body(): pl.pallas_call(functools.partial(kernel, n_dom, n_edge), out_shape=(jax.S...  81.6 us
    unnamed x4, local copies, waits for them, and re-layouts  2.88 us

profile of v2, /device:TPU:24, one launch (start us, length us, event | category | flops | bytes accessed | tf_op | source)
XLA Modules:
  0.0 85.1 jit_solution(4423459086105322775)
XLA Ops:
  0.6 81.6 %shard_map.140 = (bf16[1024,512]{1,0:T(8,128)(2,1)}, bf16[32,256]{1,0:T(8,128)(2,1)}) custom-call(s32[2,16]{1,0:T(2,128)} %bitcast.7, s32[1,1024]{1,0:T(1,128)} %bitcast.6, s32[2,1024]{1,0:T(2,128)} %ai_ref.1, bf16[32,256]{1,0:T(8,128)(2,1)} %atoms_ref.1, bf16[64,512]{1,0:T(8,128)(2,1)} %wd_ref.1, bf16[1024,512]{1,0:T(8,128)(2,1)} %edges_h.1, ...), custom_call_target="tpu_custom_call" | custom-call | tf_op jit(solution)/shard_map/pallas_call | solution.py:450
  82.2 0.0 copy-start
  82.2 2.3 %copy.17 = bf16[1024,512]{1,0:T(8,128)(2,1)} copy(bf16[1024,512]{1,0:T(8,128)(2,1)} %get-tuple-element.4) | data formatting | bytes 2097152
  84.5 0.0 copy-done
  84.5 0.6 copy.18
Async XLA Ops:
  82.2 2.3 %copy-start = (bf16[32,256]{1,0:T(8,128)(2,1)S(1)}, bf16[32,256]{1,0:T(8,128)(2,1)}, u32[]{:S(2)}) copy-start(bf16[32,256]{1,0:T(8,128)(2,1)} %get-tuple-element.5) | copy-start | bytes 49156

commit v3 on v2

--- a/solution.py
+++ b/solution.py
@@ -13,7 +13,7 @@
 BF16 = jnp.bfloat16
 F32 = jnp.float32
 I32 = jnp.int32
-CHUNKS = 8
+CHUNKS = 4
 PIECES = 16
 
 
@@ -46,11 +46,11 @@
 def kernel(
     n_dom,
     n_edge,
-    ts_ref,
-    rev_ref,
-    ai_ref,
-    atoms_ref,
-    wd_ref,
+    ts_h,
+    rev_h,
+    ai_h,
+    atoms_h,
+    wd_h,
     edges_h,
     tiles_h,
     we_h,
@@ -59,8 +59,13 @@
     wmsg_h,
     watom_h,
     wjoin_h,
-    out_ref,
     natoms_ref,
+    es_v,
+    pre_v,
+    na_v,
+    src_g,
+    tgt_g,
+    wjoin_v,
     edges_v,
     tiles_v,
     we_v,
@@ -68,7 +73,11 @@
     wres_v,
     wmsg_v,
     watom_v,
-    wjoin_v,
+    ts_ref,
+    rev_ref,
+    ai_ref,
+    atoms_ref,
+    wd_ref,
     gath,
     trip_v,
     pack_v,
@@ -79,18 +88,13 @@
     rec_v,
     keep_v,
     tgt_t,
-    src_g,
-    tgt_g,
     cols_v,
     rank_v,
-    es_v,
     msg_v,
-    pre_v,
     rs_v,
     rel_v,
     hop_v,
     fin_v,
-    na_v,
     load_sem,
     ring_send,
     ring_recv,
@@ -132,10 +136,17 @@
         load(base + 5, watom_h, watom_v),
         load(base + 6, wjoin_h, wjoin_v),
     ]
+    wd_load = load(base + 7, wd_h, wd_ref)
+    index_loads = [load(base + 8, rev_h, rev_ref), load(base + 9, ai_h, ai_ref), load(base + 10, atoms_h, atoms_ref),
+                   load(base + 11, ts_h, ts_ref)]
     we_load.start()
-    for pair in edge_loads:
-        for one in pair:
+    for c in (c for j in range(CHUNKS // 2) for c in (j, j + CHUNKS // 2)):
+        for one in edge_loads[c]:
             one.start()
+
+    wd_load.start()
+    for one in index_loads:
+        one.start()
 
     barrier = pltpu.get_barrier_semaphore()
     for peer in (left, right):
@@ -168,11 +179,14 @@
             device_id_type=MESH,
         )
 
+    wd_load.wait()
     zeros_down = jnp.zeros_like(wd_ref[...])
     wd_lo = jnp.concatenate([wd_ref[...], zeros_down], axis=0)
     wd_hi = jnp.concatenate([zeros_down, wd_ref[...]], axis=0)
+    orders = [[c for c in range(CHUNKS)], [(c + CHUNKS // 2) % CHUNKS for c in range(CHUNKS)]]
     we_load.wait()
-    for c in range(CHUNKS):
+    for j in range(CHUNKS):
+        c = orders[j % 2][j // 2]
         for one in edge_loads[c]:
             one.wait()
         x = jnp.concatenate(
@@ -181,12 +195,16 @@
         hidden = silu(dot(x, we_v[...])).astype(BF16)
         narrow = silu(dot_nt(hidden[:sub], wd_lo) + dot_nt(hidden[sub:], wd_hi)).astype(BF16)
         gath[pl.ds(me_z * groups + c * per, per)] = narrow.reshape(per, narrow.shape[0] // per, narrow.shape[1])
-        if c == 0:
+        if j == 0:
             pl.semaphore_wait(barrier, n_dom + 1)
-        ring(0, 0, c, False).start()
-        ring(1, 0, c, False).start()
+        ring(j % 2, 0, c, False).start()
+    for j in range(CHUNKS // 2, CHUNKS):
+        for direction in range(2):
+            ring(direction, 0, orders[direction][j], False).start()
 
     shift = log2(rows * n_edge)
+    for one in index_loads:
+        one.wait()
     rev_row = rev_ref[...]
     hold_row = lax.shift_right_logical(rev_row, shift)
     local_row = hold_row == me_d
@@ -196,8 +214,9 @@
     piece = rows // PIECES
 
     def forward(t):
-        s, c = 1 + lax.div(t, CHUNKS), lax.rem(t, CHUNKS)
+        s, at = 1 + lax.div(t, CHUNKS), lax.rem(t, CHUNKS)
         for direction in range(2):
+            c = at if direction == 0 else lax.rem(at + CHUNKS // 2, CHUNKS)
             ring(direction, s - 1, c, True).wait_recv()
             ring(direction, s, c, False).start()
 
@@ -210,10 +229,7 @@
         rank_v[...] = rank_v[...] + jnp.sum(flag(before), axis=0, keepdims=True)
         lower = (rev_row >= lax.shift_left(hold_col, shift)) & (rev_row < rev_col)
         rank = jnp.sum(flag(lower), axis=1, keepdims=True).astype(I32)
-        high = jnp.where(rank >= half_cap, 1, 0)
-        code = jnp.where(hold_col == me_d, -1, hold_col * half_cap + rank - high * half_cap)
-        rec_v[here] = flag(iota((piece, slots), 1) == code).astype(BF16)
-        keep_v[here] = flag((iota((piece, 128), 1) >= 64) == (high == 1))
+        cols_v[3, here] = jnp.broadcast_to(rank, (piece, 8))
 
     def select(i):
         at = i * piece
@@ -231,39 +247,60 @@
         )
         loc_v[here] = flag(iota((piece, rows), 1) == from_col).astype(BF16)
 
-    def onehots(i):
+    def receive(i, carry):
         here = pl.ds(i * piece, piece)
+        hold_col = lax.shift_right_logical(cols_v[0, here, 0:1], shift)
+        rank = cols_v[3, here, 0:1]
+        high = jnp.where(rank >= half_cap, 1, 0)
+        code = jnp.where(hold_col == me_d, -1, hold_col * half_cap + rank - high * half_cap)
+        rec_v[here] = flag(iota((piece, slots), 1) == code).astype(BF16)
+        keep_v[here] = flag((iota((piece, 128), 1) >= 64) == (high == 1))
         atom_piece = part_atoms // PIECES
         tgt_t[pl.ds(i * atom_piece, atom_piece)] = flag(
             iota((atom_piece, rows), 0) + i * atom_piece == ai_ref[1:2]
         ).astype(BF16)
+        return carry
+
+    def ends(i, carry):
+        here = pl.ds(i * piece, piece)
         lanes = iota((piece, part_atoms), 1)
         src_g[here] = flag(lanes == cols_v[1, here, 0:1]).astype(BF16)
         tgt_g[here] = flag(lanes == cols_v[2, here, 0:1]).astype(BF16)
+        return carry
 
     rank_v[...] = jnp.zeros_like(rank_v)
     middle = (steps - 2) * CHUNKS
-    for k, work in enumerate((ranks, select, onehots)):
-
-        def turn(i, carry, k=k, work=work):
-            if k * PIECES < middle:
-                forward(k * PIECES + i)
-            work(i)
-            return carry
-
-        lax.fori_loop(0, PIECES, turn, 0)
+
+    def first_turn(i, carry):
+        if middle >= PIECES // 2:
+            forward(i)
+        ranks(2 * i)
+        ranks(2 * i + 1)
+        return carry
+
+    def second_turn(i, carry):
+        if middle >= 3 * PIECES // 2:
+            forward(PIECES // 2 + i)
+        select(i)
+        return carry
+
+    assert middle in (0, PIECES // 2, 3 * PIECES // 2)
+    lax.fori_loop(0, PIECES // 2, first_turn, 0)
+    lax.fori_loop(0, PIECES, second_turn, 0)
 
     arr_v[pl.ds(me_d * half_cap, half_cap)] = jnp.zeros((half_cap, 128), BF16)
 
     last = steps - 1
     split = CHUNKS // 2
-    for c in range(CHUNKS):
+    for j in range(CHUNKS):
         for direction in range(2):
+            c = orders[direction][j]
             ring(direction, last - 1, c, True).wait_recv()
-            if (c < split) == (direction == 0):
+            if j < split:
                 ring(direction, last, c, False).start()
-    for c in range(CHUNKS):
-        ring(0 if c < split else 1, last, c, True).wait_recv()
+    for j in range(split):
+        for direction in range(2):
+            ring(direction, last, orders[direction][j], True).wait_recv()
 
     others[0].wait()
     blocks = tiles_v.shape[0]
@@ -308,6 +345,7 @@
         device_id={"dom": lax.rem(me_d + 1, n_dom)},
         device_id_type=MESH,
     )
+    lax.fori_loop(0, PIECES, receive, 0)
     part = rows // 4
     for i in range(4):
         mir_v[pl.ds(i * part, part)] = dot(loc_v[pl.ds(i * part, part)], trip_v[...])
@@ -366,25 +404,46 @@
         return pl.ds(i * own_atoms, own_atoms)
 
     hop = n_edge // 4
-    for d in range(2 * hop, hop, -1):
-        push(rs_v.at[atoms_of(away(d))], rel_v.at[slot_of(d - hop - 1)], (0, 1), away(d - hop))
-        if d < 2 * hop:
-            push(rs_v.at[atoms_of(away(-d))], rel_v.at[slot_of(d - 1)], (0, 1), away(hop - d))
+    half_own = own_atoms // 2
+
+    def half_of(device, side):
+        return pl.ds(device * own_atoms + side * half_own, half_own)
+
+    for side in range(2):
+        sign = 1 - 2 * side
+        push(
+            rs_v.at[half_of(away(sign * 2 * hop), side)],
+            rel_v.at[half_of(side * hop + hop - 1, side)],
+            (0, 1),
+            away(sign * hop),
+        )
+    for d in range(2 * hop - 1, hop, -1):
+        for side in range(2):
+            sign = 1 - 2 * side
+            push(
+                rs_v.at[atoms_of(away(sign * d))],
+                rel_v.at[slot_of(side * hop + d - hop - 1)],
+                (0, 1),
+                away(sign * (d - hop)),
+            )
     for d in range(hop - 1, 0, -1):
         push(rs_v.at[atoms_of(away(d))], fin_v.at[slot_of(d - 1)], (0, 2), away(d))
         push(rs_v.at[atoms_of(away(-d))], fin_v.at[slot_of(hop + d - 1)], (0, 2), away(-d))
+    for side in range(2):
+        rel_v[half_of(side * hop + hop - 1, 1 - side)] = jnp.zeros((half_own, atom_width), BF16)
+    lax.fori_loop(0, PIECES, ends, 0)
 
     def pre_part(i, carry):
         here = pl.ds(i * part, part)
         pre_v[here] = dot(es_v[here], wjoin_v[pl.ds(2 * atom_width, width)])
         return carry
 
-    local(rel_v, (0, 1)).wait_recv()
-    for side, first, count in ((0, 0, hop), (1, hop, hop - 1)):
+    local(rel_v.at[pl.ds(0, (2 * hop - 1) * own_atoms)], (0, 1)).wait_recv()
+    for side in range(2):
         owner = away(hop if side == 0 else -hop)
         relayed = rs_v[atoms_of(owner)].astype(F32)
-        for i in range(first, first + count):
-            relayed = relayed + rel_v[slot_of(i)].astype(F32)
+        for i in range(hop):
+            relayed = relayed + rel_v[slot_of(side * hop + i)].astype(F32)
         hop_v[slot_of(side)] = relayed.astype(BF16)
         push(hop_v.at[slot_of(side)], fin_v.at[slot_of((side + 1) * hop - 1)], (0, 2), owner)
     lax.fori_loop(0, 4, pre_part, 0)
@@ -406,19 +465,11 @@
         sign = 1 - 2 * side
         passed = na_v.at[atoms_of(away(-sign * hop))]
         local(passed, (3, 4 + side)).wait_recv()
-        for d in range(hop - side, 0, -1):
+        far = na_v.at[half_of(away(-sign * hop), side)]
+        push(far, far, (3, 6), away(sign * hop))
+        for d in range(hop - 1, 0, -1):
             push(passed, passed, (3, 6), away(sign * d))
     local(na_v.at[pl.ds(0, (n_edge - 3) * own_atoms)], (3, 6)).wait_recv()
-
-    def final_part(i, carry):
-        here = pl.ds(i * part, part)
-        ends = jnp.concatenate([dot(src_g[here], na_v[...]), dot(tgt_g[here], na_v[...])], axis=1).astype(BF16)
-        update = silu(dot(ends, wjoin_v[pl.ds(0, 2 * atom_width)]) + pre_v[here])
-        out_ref[here] = ((es_v[here].astype(F32) + update) * ROOT_HALF).astype(BF16)
-        return carry
-
-    for i in range(4):
-        final_part(i, 0)
 
     most = pl.ds(0, part_atoms - own_atoms)
     local(rs_v.at[most], (0, 1)).wait_send()
@@ -430,8 +481,25 @@
         return carry
 
     lax.fori_loop(0, last * CHUNKS, drain, 0)
-    for c in range(CHUNKS):
-        ring(0 if c < split else 1, last, c, False).wait_send()
+    for j in range(split):
+        for direction in range(2):
+            ring(direction, last, orders[direction][j], False).wait_send()
+
+
+def finish(fresh_ref, es_ref, pre_ref, na_ref, src_ref, tgt_ref, wjoin_ref, out_h, natoms_ref, out_v, sem):
+    rows = es_ref.shape[0]
+    part = rows // 4
+    natoms_ref[...] = fresh_ref[...]
+    copies = []
+    for i in range(4):
+        here = pl.ds(i * part, part)
+        ends = jnp.concatenate([dot(src_ref[here], na_ref[...]), dot(tgt_ref[here], na_ref[...])], axis=1).astype(BF16)
+        update = silu(dot(ends, wjoin_ref[pl.ds(0, 2 * na_ref.shape[1])]) + pre_ref[here])
+        out_v[here] = ((es_ref[here].astype(F32) + update) * ROOT_HALF).astype(BF16)
+        copies.append(pltpu.make_async_copy(out_v.at[here], out_h.at[here], sem.at[i]))
+        copies[-1].start()
+    for one in copies:
+        one.wait()
 
 
 def body(n_dom, n_edge, edges, atoms, reverse, atom_index, tile_source, tiles, weight_edge, weight_down, weight_up,
@@ -446,15 +514,20 @@
     capacity = rows // n_dom
     slots = n_dom * capacity // 2
     vmem = pl.BlockSpec(memory_space=pltpu.VMEM)
-    hbm = pl.BlockSpec(memory_space=pl.ANY)
-    return pl.pallas_call(
+    hbm = pl.BlockSpec(memory_space=pltpu.HBM)
+    fresh, state, pre, everyone, src_hot, tgt_hot, join = pl.pallas_call(
         functools.partial(kernel, n_dom, n_edge),
         out_shape=(
+            jax.ShapeDtypeStruct((own_atoms, atom_width), BF16),
             jax.ShapeDtypeStruct((rows, width), BF16),
-            jax.ShapeDtypeStruct((own_atoms, atom_width), BF16),
+            jax.ShapeDtypeStruct((rows, width), F32),
+            jax.ShapeDtypeStruct((part_atoms, atom_width), BF16),
+            jax.ShapeDtypeStruct((rows, part_atoms), BF16),
+            jax.ShapeDtypeStruct((rows, part_atoms), BF16),
+            jax.ShapeDtypeStruct(weight_join.shape, BF16),
         ),
-        in_specs=[pl.BlockSpec(memory_space=pltpu.SMEM)] + [vmem] * 4 + [hbm] * 8,
-        out_specs=(vmem, vmem),
+        in_specs=[hbm] * 13,
+        out_specs=(vmem,) * 7,
         scratch_shapes=[
             pltpu.VMEM((rows, width), BF16),
             pltpu.VMEM(tiles.shape, BF16),
@@ -463,7 +536,11 @@
             pltpu.VMEM((2, width, width), BF16),
             pltpu.VMEM(weight_message.shape, BF16),
             pltpu.VMEM(weight_atom.shape, BF16),
-            pltpu.VMEM(weight_join.shape, BF16),
+            pltpu.SMEM(tile_source.shape[::-1], I32),
+            pltpu.VMEM((1, rows), I32),
+            pltpu.VMEM((2, rows), I32),
+            pltpu.VMEM((own_atoms, atom_width), BF16),
+            pltpu.VMEM(weight_down.shape, BF16),
             pltpu.VMEM((n_edge * groups, 64, 128), BF16),
             pltpu.VMEM((rows, 128), BF16),
             pltpu.VMEM((slots, 128), BF16),
@@ -474,42 +551,53 @@
             pltpu.VMEM((rows, slots), BF16),
             pltpu.VMEM((rows, 128), F32),
             pltpu.VMEM((part_atoms, rows), BF16),
-            pltpu.VMEM((rows, part_atoms), BF16),
-            pltpu.VMEM((rows, part_atoms), BF16),
-            pltpu.VMEM((3, rows, 8), I32),
+            pltpu.VMEM((4, rows, 8), I32),
             pltpu.VMEM((8, rows), F32),
-            pltpu.VMEM((rows, width), BF16),
             pltpu.VMEM((rows, atom_width), BF16),
-            pltpu.VMEM((rows, width), F32),
             pltpu.VMEM((part_atoms, atom_width), BF16),
-            pltpu.VMEM((part_atoms // 2 - own_atoms, atom_width), BF16),
+            pltpu.VMEM((part_atoms // 2, atom_width), BF16),
             pltpu.VMEM((2 * own_atoms, atom_width), BF16),
             pltpu.VMEM((part_atoms // 2, atom_width), BF16),
-            pltpu.VMEM((part_atoms, atom_width), BF16),
-            pltpu.SemaphoreType.DMA((2 * CHUNKS + 7,)),
+            pltpu.SemaphoreType.DMA((2 * CHUNKS + 12,)),
             pltpu.SemaphoreType.DMA((2, n_edge // 2, CHUNKS)),
             pltpu.SemaphoreType.DMA((2, n_edge // 2, CHUNKS)),
             pltpu.SemaphoreType.DMA((2,)),
             pltpu.SemaphoreType.DMA((7,)),
         ],
         compiler_params=pltpu.CompilerParams(
-            collective_id=0, has_side_effects=True, vmem_limit_bytes=56 * 1024 * 1024
+            collective_id=0, has_side_effects=True, vmem_limit_bytes=34 * 1024 * 1024
         ),
     )(
-        tile_source.T,
-        reverse.reshape(1, rows),
-        atom_index,
-        atoms,
-        weight_down,
-        edges,
-        tiles,
-        weight_edge,
-        weight_up.reshape(2 * channels, width),
-        weight_residual.reshape(2, width, width),
-        weight_message,
-        weight_atom,
-        weight_join,
+        *(
+            pltpu.with_memory_space_constraint(one, pltpu.HBM)
+            for one in (
+                tile_source.T,
+                reverse.reshape(1, rows),
+                atom_index,
+                atoms,
+                weight_down,
+                edges,
+                tiles,
+                weight_edge,
+                weight_up.reshape(2 * channels, width),
+                weight_residual.reshape(2, width, width),
+                weight_message,
+                weight_atom,
+                weight_join,
+            )
+        ),
     )
+    return pl.pallas_call(
+        finish,
+        out_shape=(
+            jax.ShapeDtypeStruct((rows, width), BF16),
+            jax.ShapeDtypeStruct((own_atoms, atom_width), BF16),
+        ),
+        in_specs=[vmem] * 7,
+        out_specs=(hbm, vmem),
+        scratch_shapes=[pltpu.VMEM((rows, width), BF16), pltpu.SemaphoreType.DMA((4,))],
+        compiler_params=pltpu.CompilerParams(vmem_limit_bytes=12 * 1024 * 1024),
+    )(fresh, state, pre, everyone, src_hot, tgt_hot, join)
 
 
 def solution(mesh):

time: 85.3 us -> 78 us (0.914)
  Pallas kernels: 81.6 us -> 77.3 us
  local copies, waits for them, and re-layouts: 2.88 us -> 0 us
    pallas_call x1, Pallas kernels: 81.6 us -> 74.2 us  [body(): pl.pallas_call(functools.partial(kernel, n_dom, n_edge), out_shape=(jax.S...]
    pallas_call x0 -> x1, Pallas kernels: none -> 3.1 us  [body(): pl.pallas_call(finish, out_shape=(jax.ShapeDtypeStruct((rows, width), BF1...]
    unnamed x4 -> x0, local copies, waits for them, and re-layouts: 2.88 us -> none
where the time goes in v3:
time: 78 us; the launch traced here: 77.9 us
  Pallas kernels  77.3 us (99%)
    pallas_call x1, Pallas kernels, body(): pl.pallas_call(functools.partial(kernel, n_dom, n_edge), out_shape=(jax.S...  74.2 us
    pallas_call x1, Pallas kernels, body(): pl.pallas_call(finish, out_shape=(jax.ShapeDtypeStruct((rows, width), BF1...  3.1 us

profile of v3, /device:TPU:24, one launch (start us, length us, event | category | flops | bytes accessed | tf_op | source)
XLA Modules:
  0.0 77.9 jit_solution(16724005336265592257)
XLA Ops:
  0.6 74.2 %shard_map.140 = (bf16[32,256]{1,0:T(8,128)(2,1)S(1)}, bf16[1024,512]{1,0:T(8,128)(2,1)S(1)}, f32[1024,512]{1,0:T(8,128)S(1)}, bf16[512,256]{1,0:T(8,128)(2,1)S(...) custom-call(s32[2,16]{1,0:T(2,128)} %bitcast.7, ...), custom_call_target="tpu_custom_call" | custom-call | tf_op jit(solution)/shard_map/pallas_call | solution.py:518
  74.8 3.1 %shard_map.141 = (bf16[1024,512]{1,0:T(8,128)(2,1)}, bf16[32,256]{1,0:T(8,128)(2,1)}) custom-call(bf16[32,256]{1,0:T(8,128)(2,1)S(1)} %get-tuple-element.9.fresh_ref, bf16[1024,512]{1,0:T(8,128)(2,1)S(1)} %get-tuple-element.10.es_ref, f32[1024,512]{1,0:T(8,128)S(1)} %get-tuple-element.11.pre_ref, bf16[512,256]{1,0:T(8,128)(2,1)S(1)} %get-tuple-element.12.na_ref, ...), custom_call_target="tpu_custom_call" | custom-call | tf_op jit(solution)/shard_map/pallas_call | solution.py:590

commit v4 on v3

--- a/solution.py
+++ b/solution.py
@@ -353,7 +353,9 @@
         one.wait()
     exchange.wait()
 
-    def edge_part(i, carry):
+    part = rows // 2
+
+    def edge_part(i):
         here = pl.ds(i * part, part)
         found = dot(rec_v[here], arr_v[...]) * keep_v[here]
         mirrored = (found + pltpu.roll(found, 64, 1) + mir_v[here]).astype(BF16)
@@ -364,10 +366,9 @@
         state = ((state.astype(F32) + branch) * ROOT_HALF).astype(BF16)
         es_v[here] = state
         msg_v[here] = dot(state, wmsg_v[...]).astype(BF16)
-        return carry
-
-    for i in range(4):
-        edge_part(i, 0)
+
+    for i in range(2):
+        edge_part(i)
 
     a_part = part_atoms // 4
     for i in range(4):
@@ -434,7 +435,7 @@
     lax.fori_loop(0, PIECES, ends, 0)
 
     def pre_part(i, carry):
-        here = pl.ds(i * part, part)
+        here = pl.ds(i * (rows // 4), rows // 4)
         pre_v[here] = dot(es_v[here], wjoin_v[pl.ds(2 * atom_width, width)])
         return carry
 

time: 78 us -> 77.2 us (0.990)
  Pallas kernels: 77.3 us -> 76.5 us
    pallas_call x1, Pallas kernels: 74.2 us -> 73.4 us  [body(): pl.pallas_call(functools.partial(kernel, n_dom, n_edge), out_shape=(jax.S...]
where the time goes in v4:
time: 77.2 us; the launch traced here: 77.1 us
  Pallas kernels  76.5 us (99%)
    pallas_call x1, Pallas kernels, body(): pl.pallas_call(functools.partial(kernel, n_dom, n_edge), out_shape=(jax.S...  73.4 us
    pallas_call x1, Pallas kernels, body(): pl.pallas_call(finish, out_shape=(jax.ShapeDtypeStruct((rows, width), BF1...  3.1 us

profile of v4, /device:TPU:24, one launch (start us, length us, event | category | flops | bytes accessed | tf_op | source)
XLA Modules:
  0.0 77.1 jit_solution(13890006934749757328)
XLA Ops:
  0.6 73.4 %shard_map.140 = (bf16[32,256]{1,0:T(8,128)(2,1)S(1)}, bf16[1024,512]{1,0:T(8,128)(2,1)S(1)}, f32[1024,512]{1,0:T(8,128)S(1)}, bf16[512,256]{1,0:T(8,128)(2,1)S(...) custom-call(s32[2,16]{1,0:T(2,128)} %bitcast.7, ...), custom_call_target="tpu_custom_call" | custom-call | tf_op jit(solution)/shard_map/pallas_call | solution.py:519
  74.0 3.1 %shard_map.141 = (bf16[1024,512]{1,0:T(8,128)(2,1)}, bf16[32,256]{1,0:T(8,128)(2,1)}) custom-call(bf16[32,256]{1,0:T(8,128)(2,1)S(1)} %get-tuple-element.9.fresh_ref, bf16[1024,512]{1,0:T(8,128)(2,1)S(1)} %get-tuple-element.10.es_ref, f32[1024,512]{1,0:T(8,128)S(1)} %get-tuple-element.11.pre_ref, bf16[512,256]{1,0:T(8,128)(2,1)S(1)} %get-tuple-element.12.na_ref, ...), custom_call_target="tpu_custom_call" | custom-call | tf_op jit(solution)/shard_map/pallas_call | solution.py:591
